TPU v7x, 256 devices: a whole 4x4x8 slice. The times are simulated.
256 devices in a mesh: row: 8 (over x, core), col: 32 (over y, z).
Axes of the slice: x: 4, y: 4, z: 8, core: 2. Of those that a mesh axis runs over, the one named last changes fastest.
Arguments:
- frames: bfloat16 [3072, 4096], P('row', 'col'), may hold values from -6 to 6
- gain: float32 [4096], replicated, may hold values from 0.3 to 10
- w_value: bfloat16 [4096, 4096], P('row', 'col'), may hold values from -0.09375 to 0.09375
- w_gate: bfloat16 [4096, 4096], P('row', 'col'), may hold values from -0.09375 to 0.09375
- kernel: float32 [31, 4096], P(None, 'col'), may hold values from -1.5 to 1.5
- bias: float32 [4096], P('col'), may hold values from -3 to 3
- w_out: bfloat16 [4096, 4096], P('row', 'col'), may hold values from -0.09375 to 0.09375
- grad_out: bfloat16 [3072, 4096], P('row', 'col'), may hold values from -6 to 6
Outputs:
- encoded: bfloat16 [3072, 4096], P('row', 'col')
- input_grad: bfloat16 [3072, 4096], P('row', 'col')
- grad_value: float32 [4096, 4096], P('row', 'col')
- grad_gate: float32 [4096, 4096], P('row', 'col')
- grad_kernel: float32 [31, 4096], P(None, 'col')
- grad_bias: float32 [4096], P('col')
- grad_out_weight: float32 [4096, 4096], P('row', 'col')
- grad_gain: float32 [4096], P('col')
All inputs are finite; a program needn't handle non-finite values.
Results may differ from a plain program's by a relative error of at most 0.035.
Values may be sent and summed in bfloat16 or wider, within the bound.
No kernel may reach another device: no remote copies, remote signals or barrier semaphores. Data moves between devices by JAX's collectives and lax.ppermute only.
A program may use at most 128 MiB of HBM per device.

v0:
```python
import jax
import jax.numpy as jnp
from jax import lax
from jax.sharding import PartitionSpec as P

K = 31
LEN = 2048
epsilon = 1e-05


def extended(block, sides, width):
    for axis, dim in sides:
        count = lax.axis_size(axis)
        forward = [(i, i + 1) for i in range(count - 1)]
        backward = [(target, source) for source, target in forward]
        low = lax.ppermute(
            lax.slice_in_dim(block, block.shape[dim] - width, None, axis=dim), axis, forward
        )
        high = lax.ppermute(lax.slice_in_dim(block, 0, width, axis=dim), axis, backward)
        block = jnp.concatenate([low, block, high], axis=dim)
    return block


def tap_masks(positions):
    offsets = jnp.arange(K, dtype=jnp.int32) - K // 2
    placed = (positions % LEN)[None, :] + offsets[:, None]
    return ((placed >= 0) & (placed < LEN)).astype(jnp.float32)


def contract_rows(left, right):
    return lax.dot_general(
        left, right, (((0,), (0,)), ((), ())), preferred_element_type=jnp.float32
    )


def contract_cols(left, right):
    return lax.dot_general(
        left, right, (((1,), (1,)), ((), ())), preferred_element_type=jnp.float32
    )


def shards(frames, gain, w_value, w_gate, kernel, bias, w_out, grad_out):
    row_count = frames.shape[0]
    col_count = frames.shape[1]
    chan_count = w_value.shape[1]
    width = col_count * lax.axis_size("col")
    half_width = K // 2
    row_start = lax.axis_index("row") * row_count
    col_start = lax.axis_index("col") * col_count
    local_gain = lax.dynamic_slice_in_dim(gain, col_start, col_count, 0)
    wide = frames.astype(jnp.float32)
    sum_row, square_sum = lax.psum((jnp.sum(wide, axis=1), jnp.sum(wide * wide, axis=1)), "col")
    mean_row = sum_row / width
    inv_std = lax.rsqrt(square_sum / width - mean_row * mean_row + epsilon)
    centred = (wide - mean_row[:, None]) * inv_std[:, None]
    normed = lax.all_gather(
        (centred * local_gain[None, :]).astype(jnp.bfloat16), "col", axis=1, tiled=True
    )
    value_full, gate_full = (
        lax.all_gather(w_value, "row", axis=0, tiled=True),
        lax.all_gather(w_gate, "row", axis=0, tiled=True),
    )
    value_pre = jnp.dot(normed, value_full, preferred_element_type=jnp.float32)
    gate_pre = jnp.dot(normed, gate_full, preferred_element_type=jnp.float32)
    gate_sig = jax.nn.sigmoid(gate_pre)
    gated = (value_pre * gate_sig).astype(jnp.bfloat16)
    padded_glu = extended(gated, (("row", 0),), half_width).astype(jnp.float32)
    local_masks = tap_masks(row_start + jnp.arange(row_count, dtype=jnp.int32))
    conv_pre = jnp.zeros((row_count, chan_count), jnp.float32) + bias[None, :]
    for tap_index in range(K):
        conv_pre = (
            conv_pre
            + kernel[tap_index][None, :]
            * local_masks[tap_index][:, None]
            * padded_glu[tap_index : tap_index + row_count]
        )
    conv_sig = jax.nn.sigmoid(conv_pre)
    activated = (conv_pre * conv_sig).astype(jnp.bfloat16)
    act_full = lax.all_gather(activated, "col", axis=1, tiled=True)
    out_full = lax.all_gather(w_out, "row", axis=0, tiled=True)
    encoded = (
        frames.astype(jnp.float32) + jnp.dot(act_full, out_full, preferred_element_type=jnp.float32)
    ).astype(jnp.bfloat16)
    act_terms = contract_cols(grad_out, out_full)
    act_grad = lax.psum_scatter(
        act_terms.astype(jnp.bfloat16), "col", scatter_dimension=1, tiled=True
    ).astype(jnp.float32)
    grad_out_weight = lax.psum_scatter(
        contract_rows(act_full, grad_out).astype(jnp.bfloat16),
        "row",
        scatter_dimension=0,
        tiled=True,
    ).astype(jnp.float32)
    conv_grad = (act_grad * conv_sig * (1.0 + conv_pre * (1.0 - conv_sig))).astype(jnp.bfloat16)
    conv_wide = conv_grad.astype(jnp.float32)
    padded_grad = extended(conv_grad, (("row", 0),), half_width).astype(jnp.float32)
    outer_masks = tap_masks(
        row_start - half_width + jnp.arange(row_count + 2 * half_width, dtype=jnp.int32)
    )
    glu_grad = jnp.zeros((row_count, chan_count), jnp.float32)
    kernel_rows = []
    for tap_index in range(K):
        begin = 2 * half_width - tap_index
        glu_grad = (
            glu_grad
            + kernel[tap_index][None, :]
            * outer_masks[tap_index, begin : begin + row_count][:, None]
            * padded_grad[begin : begin + row_count]
        )
        kernel_rows.append(
            jnp.sum(
                local_masks[tap_index][:, None]
                * conv_wide
                * padded_glu[tap_index : tap_index + row_count],
                axis=0,
            )
        )
    kernel_term = jnp.stack(kernel_rows)
    bias_term = jnp.sum(conv_wide, axis=0)
    grad_kernel, grad_bias = lax.psum((kernel_term, bias_term), "row")
    value_grad = (glu_grad * gate_sig).astype(jnp.bfloat16)
    gate_grad = (glu_grad * value_pre * gate_sig * (1.0 - gate_sig)).astype(jnp.bfloat16)
    both_grads = jnp.concatenate([value_grad, gate_grad], axis=1)
    in_weight = lax.psum_scatter(
        contract_rows(normed, both_grads).astype(jnp.bfloat16),
        "row",
        scatter_dimension=0,
        tiled=True,
    ).astype(jnp.float32)
    grad_value = in_weight[:, :chan_count]
    grad_gate = in_weight[:, chan_count:]
    norm_terms = contract_cols(value_grad, value_full) + contract_cols(gate_grad, gate_full)
    normed_grad = lax.psum_scatter(
        norm_terms.astype(jnp.bfloat16), "col", scatter_dimension=1, tiled=True
    ).astype(jnp.float32)
    hat_grad = normed_grad * local_gain[None, :]
    first_sum, second_sum = lax.psum(
        (jnp.sum(hat_grad, axis=1), jnp.sum(hat_grad * centred, axis=1)), "col"
    )
    input_grad = (
        grad_out.astype(jnp.float32)
        + inv_std[:, None]
        * (hat_grad - first_sum[:, None] / width - centred * (second_sum / width)[:, None])
    ).astype(jnp.bfloat16)
    gain_term = jnp.sum(normed_grad * centred, axis=0)
    grad_gain = lax.psum(gain_term, "row")
    return (
        encoded,
        input_grad,
        grad_value,
        grad_gate,
        grad_kernel,
        grad_bias,
        grad_out_weight,
        grad_gain,
    )


def solution(mesh):
    placed = (
        P("row", "col"),
        P(),
        P("row", "col"),
        P("row", "col"),
        P(None, "col"),
        P("col"),
        P("row", "col"),
        P("row", "col"),
    )
    return jax.shard_map(
        shards,
        mesh=mesh,
        in_specs=placed,
        out_specs=(
            P("row", "col"),
            P("row", "col"),
            P("row", "col"),
            P("row", "col"),
            P(None, "col"),
            P("col"),
            P("row", "col"),
            P("col"),
        ),
        check_vma=False,
    )
```

profile of v0, /device:TPU:0, one launch (start us, length us, event | category | flops | bytes accessed | tf_op | source)
XLA Modules:
  0.0 864.5 jit_solution(822775014375690964)
XLA Ops:
  7.2 0.7 all-gather.14.cloned.1.call-update
  7.9 0.7 all-gather.10.cloned.1.call-update
  8.7 0.8 dynamic_slice.3
  9.5 1.1 convert_reduce_fusion.1
  10.5 76.2 %all-reduce.1 = (f32[384]{0:T(512)S(1)}, f32[384]{0:T(512)S(1)}) all-reduce(f32[384]{0:T(512)S(1)} %get-tuple-element.44, f32[384]{0:T(512)S(1)} %get-tuple-element.43), channel_id=1, replica_groups=mesh['row'=8,'col'=32] {'col'}, use_global_device_ids=true, to_apply=%region_3.0 | all-reduce | flops 768 | bytes 6144 | tf_op jit(solution)/shard_map/psum | solution.py:52
  86.8 0.6 copy-done.9
  87.3 1.7 fusion.16
  89.1 0.5 all-gather.8.cloned.1.call-update
  89.7 2.3 convolution_convert_fusion
  92.0 2.8 copy.16
  95.0 0.4 copy-done.69
  95.6 0.6 slice_bitcast_fusion.29
  96.2 0.7 slice_bitcast_fusion.30
  96.9 64.5 %all-gather.6.cloned.1.call-done = bf16[384,4096]{1,0:T(8,128)(2,1)} async-done(((bf16[384,128]{1,0:T(8,128)(2,1)}), bf16[384,4096]{1,0:T(8,128)(2,1)}) %all-gather.6.cloned.1.call-update) | async-done | bytes 3145744 | tf_op jit(solution)/shard_map/all_gather | solution.py:56
  161.4 3.3 fusion.2
  164.8 24.6 %all-gather.8.cloned.1.call-done = bf16[4096,128]{1,0:T(8,128)(2,1)} async-done(((bf16[512,128]{1,0:T(8,128)(2,1)}), bf16[4096,128]{1,0:T(8,128)(2,1)}) %all-gather.8.cloned.1.call-update) | async-done | bytes 1048592 | tf_op jit(solution)/shard_map/all_gather | solution.py:60
  189.4 2.9 multiply_convert_fusion.4
  192.3 2.2 collective-permute-start
  194.4 1.3 collective-permute-start.1
  195.9 1.6 collective-permute-done.1
  197.5 215.0 %reduce-scatter.13.cloned.1.call-done = bf16[128,384]{1,0:T(8,128)(2,1)} async-done(((bf16[4096,384]{1,0:T(8,128)(2,1)}), bf16[128,384]{1,0:T(8,128)(2,1)}) %reduce-scatter.13.cloned.1.call-update) | async-done | bytes 98320
  412.5 1.0 copy.17
  414.0 4.1 fusion.75
  418.1 0.7 multiply_convert_fusion.3
  419.2 1.3 collective-permute-start.2
  420.5 1.3 collective-permute-start.3
  421.9 3.3 collective-permute-done.3
  425.6 3.1 multiply_convert_fusion
  428.7 2.6 convolution_convert_fusion.1
  431.4 1.0 fusion.124
  432.7 1.0 add_convert_fusion
  433.6 2.9 copy.18
  436.8 58.9 %all-gather.12.cloned.1.call-done = bf16[384,4096]{1,0:T(8,128)(2,1)} async-done(((bf16[384,128]{1,0:T(8,128)(2,1)}), bf16[384,4096]{1,0:T(8,128)(2,1)}) %all-gather.12.cloned.1.call-update) | async-done | bytes 3145744 | tf_op jit(solution)/shard_map/all_gather | solution.py:79
  495.7 3.9 convolution_convert_fusion.2
  499.7 1.7 fusion.73
  501.4 1.9 fusion.77
  503.3 1.9 fusion.79
  505.1 3.0 stack.127
  508.1 26.7 %reduce-scatter.9.cloned.1.call-done = bf16[512,256]{1,0:T(8,128)(2,1)} async-done(((bf16[4096,256]{1,0:T(8,128)(2,1)}), bf16[512,256]{1,0:T(8,128)(2,1)}) %reduce-scatter.9.cloned.1.call-update) | async-done | bytes 262160 | tf_op jit(solution)/shard_map/reduce_scatter | solution.py:124
  534.8 1.8 fusion.121
  536.6 2.9 fusion.3
  539.5 218.2 %reduce-scatter.15.cloned.1.call-done = bf16[128,384]{1,0:T(8,128)(2,1)} async-done(((bf16[4096,384]{1,0:T(8,128)(2,1)}), bf16[128,384]{1,0:T(8,128)(2,1)}) %reduce-scatter.15.cloned.1.call-update) | async-done | bytes 98320
  757.7 1.0 copy.19
  758.7 0.3 fusion.12
  759.0 72.2 %all-reduce = (f32[384]{0:T(512)S(1)}, f32[384]{0:T(512)S(1)}) all-reduce(f32[384]{0:T(512)S(1)} %get-tuple-element.40, f32[384]{0:T(512)S(1)} %get-tuple-element.41), channel_id=1, replica_groups=mesh['row'=8,'col'=32] {'col'}, use_global_device_ids=true, to_apply=%region_9.10 | all-reduce | flops 768 | bytes 6144 | tf_op jit(solution)/shard_map/psum | solution.py:137
  831.2 24.2 %all-reduce.2 = (f32[31,128]{1,0:T(8,128)}, f32[128]{0:T(128)}, f32[128]{0:T(128)}) all-reduce(f32[31,128]{1,0:T(8,128)S(1)} %stack.127, f32[128]{0:T(128)S(1)} %copy-done.71, f32[128]{0:T(128)S(1)} %get-tuple-element.39), channel_id=1, replica_groups=mesh['row'=8,'col'=32] {'row'}, use_global_device_ids=true, to_apply=%region_42.43 | all-reduce | flops 4224 | bytes 33792 | tf_op jit(solution)/shard_map/psum | solution.py:120
  855.4 0.9 fusion.10
  856.3 1.6 convert_element_type.92
  (178 shorter events, 2.0 us)
Async XLA Ops:
  7.2 82.6 %all-gather.14.cloned.1.call-start = ((), (), s32[]{:S(2)}) async-start(), calls=%async_computation.8 | async-start | bytes 1179648 | tf_op jit(solution)/shard_map/all_gather | solution.py:80
  7.9 89.0 %all-gather.10.cloned.1.call-start = ((), (), s32[]{:S(2)}) async-start(), calls=%async_computation.6 | async-start | bytes 1179648 | tf_op jit(solution)/shard_map/all_gather | solution.py:61
  8.7 152.8 %all-gather.6.cloned.1.call-start = ((), (), s32[]{:S(2)}) async-start(), calls=%async_computation.4 | async-start | bytes 3244032 | tf_op jit(solution)/shard_map/all_gather | solution.py:56
  9.5 80.2 %copy-start.36 = (f32[128]{0:T(128)}, f32[128]{0:T(128)S(1)}, u32[]{:S(2)}) copy-start(f32[128]{0:T(128)S(1)} %dynamic_slice.3) | copy-start | bytes 1540
  89.1 100.3 %all-gather.8.cloned.1.call-start = ((), (), s32[]{:S(2)}) async-start(), calls=%async_computation.5 | async-start | bytes 1179648 | tf_op jit(solution)/shard_map/all_gather | solution.py:60
  89.6 322.9 %reduce-scatter.13.cloned.1.call-start = ((), (), s32[]{:S(2)}) async-start(), calls=%async_computation.11 | async-start | bytes 3244032
  94.8 400.9 %all-gather.12.cloned.1.call-start = ((), (), s32[]{:S(2)}) async-start(), calls=%async_computation.7 | async-start | bytes 3244032 | tf_op jit(solution)/shard_map/all_gather | solution.py:79
  95.5 318.0 %copy-start.13 = (f32[384]{0:T(512)}, f32[384]{0:T(512)S(1)}, u32[]{:S(2)}) copy-start(f32[384]{0:T(512)S(1)} %get-tuple-element.77) | copy-start | bytes 4612
  95.5 318.0 %copy-start.14 = (f32[384]{0:T(512)}, f32[384]{0:T(512)S(1)}, u32[]{:S(2)}) copy-start(f32[384]{0:T(512)S(1)} %get-tuple-element.78) | copy-start | bytes 4612
  95.5 318.0 %copy-start.15 = (f32[384]{0:T(512)}, f32[384]{0:T(512)S(1)}, u32[]{:S(2)}) copy-start(f32[384]{0:T(512)S(1)} %get-tuple-element.91) | copy-start | bytes 4612
  95.5 318.0 %copy-start.16 = (f32[384]{0:T(512)}, f32[384]{0:T(512)S(1)}, u32[]{:S(2)}) copy-start(f32[384]{0:T(512)S(1)} %get-tuple-element.92) | copy-start | bytes 4612
  95.5 318.0 %copy-start.17 = (f32[384]{0:T(512)}, f32[384]{0:T(512)S(1)}, u32[]{:S(2)}) copy-start(f32[384]{0:T(512)S(1)} %get-tuple-element.93) | copy-start | bytes 4612
  95.5 318.0 %copy-start.18 = (f32[384]{0:T(512)}, f32[384]{0:T(512)S(1)}, u32[]{:S(2)}) copy-start(f32[384]{0:T(512)S(1)} %get-tuple-element.94) | copy-start | bytes 4612
  95.5 318.0 %copy-start.19 = (f32[384]{0:T(512)}, f32[384]{0:T(512)S(1)}, u32[]{:S(2)}) copy-start(f32[384]{0:T(512)S(1)} %get-tuple-element.76) | copy-start | bytes 4612
  95.6 318.0 %copy-start.20 = (f32[384]{0:T(512)}, f32[384]{0:T(512)S(1)}, u32[]{:S(2)}) copy-start(f32[384]{0:T(512)S(1)} %get-tuple-element.80) | copy-start | bytes 4612
  95.6 318.0 %copy-start.21 = (f32[384]{0:T(512)}, f32[384]{0:T(512)S(1)}, u32[]{:S(2)}) copy-start(f32[384]{0:T(512)S(1)} %get-tuple-element.81) | copy-start | bytes 4612
  95.6 318.0 %copy-start.22 = (f32[384]{0:T(512)}, f32[384]{0:T(512)S(1)}, u32[]{:S(2)}) copy-start(f32[384]{0:T(512)S(1)} %get-tuple-element.82) | copy-start | bytes 4612
  96.2 317.4 %copy-start.38 = (f32[128]{0:T(128)}, f32[128]{0:T(128)S(1)}, u32[]{:S(2)}) copy-start(f32[128]{0:T(128)S(1)} %get-tuple-element.143) | copy-start | bytes 1540
  96.2 317.4 %copy-start.39 = (f32[128]{0:T(128)}, f32[128]{0:T(128)S(1)}, u32[]{:S(2)}) copy-start(f32[128]{0:T(128)S(1)} %get-tuple-element.144) | copy-start | bytes 1540
  96.2 317.4 %copy-start.40 = (f32[128]{0:T(128)}, f32[128]{0:T(128)S(1)}, u32[]{:S(2)}) copy-start(f32[128]{0:T(128)S(1)} %get-tuple-element.145) | copy-start | bytes 1540
  96.2 317.4 %copy-start.41 = (f32[128]{0:T(128)}, f32[128]{0:T(128)S(1)}, u32[]{:S(2)}) copy-start(f32[128]{0:T(128)S(1)} %get-tuple-element.146) | copy-start | bytes 1540
  96.2 317.4 %copy-start.42 = (f32[128]{0:T(128)}, f32[128]{0:T(128)S(1)}, u32[]{:S(2)}) copy-start(f32[128]{0:T(128)S(1)} %get-tuple-element.147) | copy-start | bytes 1540
  192.3 3.7 collective-permute-start
  194.4 3.1 collective-permute-start.1
  195.8 222.2 %copy-start.23 = (f32[384]{0:T(512)}, f32[384]{0:T(512)S(1)}, u32[]{:S(2)}) copy-start(f32[384]{0:T(512)S(1)} %get-tuple-element.95) | copy-start | bytes 4612
  195.8 222.2 %copy-start.24 = (f32[384]{0:T(512)}, f32[384]{0:T(512)S(1)}, u32[]{:S(2)}) copy-start(f32[384]{0:T(512)S(1)} %get-tuple-element.100) | copy-start | bytes 4612
  195.8 222.2 %copy-start.25 = (f32[384]{0:T(512)}, f32[384]{0:T(512)S(1)}, u32[]{:S(2)}) copy-start(f32[384]{0:T(512)S(1)} %get-tuple-element.101) | copy-start | bytes 4612
  195.8 222.2 %copy-start.26 = (f32[384]{0:T(512)}, f32[384]{0:T(512)S(1)}, u32[]{:S(2)}) copy-start(f32[384]{0:T(512)S(1)} %get-tuple-element.102) | copy-start | bytes 4612
  195.8 222.2 %copy-start.27 = (f32[384]{0:T(512)}, f32[384]{0:T(512)S(1)}, u32[]{:S(2)}) copy-start(f32[384]{0:T(512)S(1)} %get-tuple-element.103) | copy-start | bytes 4612
  195.8 222.2 %copy-start.28 = (f32[384]{0:T(512)}, f32[384]{0:T(512)S(1)}, u32[]{:S(2)}) copy-start(f32[384]{0:T(512)S(1)} %get-tuple-element.104) | copy-start | bytes 4612
  195.8 222.2 %copy-start.29 = (f32[384]{0:T(512)}, f32[384]{0:T(512)S(1)}, u32[]{:S(2)}) copy-start(f32[384]{0:T(512)S(1)} %get-tuple-element.105) | copy-start | bytes 4612
  195.9 222.2 %copy-start.30 = (f32[384]{0:T(512)}, f32[384]{0:T(512)S(1)}, u32[]{:S(2)}) copy-start(f32[384]{0:T(512)S(1)} %get-tuple-element.106) | copy-start | bytes 4612
  195.9 222.2 %copy-start.31 = (f32[384]{0:T(512)}, f32[384]{0:T(512)S(1)}, u32[]{:S(2)}) copy-start(f32[384]{0:T(512)S(1)} %get-tuple-element.96) | copy-start | bytes 4612
  195.9 222.2 %copy-start.32 = (f32[384]{0:T(512)}, f32[384]{0:T(512)S(1)}, u32[]{:S(2)}) copy-start(f32[384]{0:T(512)S(1)} %get-tuple-element.97) | copy-start | bytes 4612
  195.9 222.2 %copy-start.33 = (f32[384]{0:T(512)}, f32[384]{0:T(512)S(1)}, u32[]{:S(2)}) copy-start(f32[384]{0:T(512)S(1)} %get-tuple-element.98) | copy-start | bytes 4612
  195.9 222.2 %copy-start.34 = (f32[384]{0:T(512)}, f32[384]{0:T(512)S(1)}, u32[]{:S(2)}) copy-start(f32[384]{0:T(512)S(1)} %get-tuple-element.99) | copy-start | bytes 4612
  418.9 116.0 %reduce-scatter.9.cloned.1.call-start = ((), (), s32[]{:S(2)}) async-start(), calls=%async_computation.9 | async-start | bytes 2359296 | tf_op jit(solution)/shard_map/reduce_scatter | solution.py:124
  419.2 2.7 collective-permute-start.2
  420.5 4.8 collective-permute-start.3
  431.4 326.3 %reduce-scatter.15.cloned.1.call-start = ((), (), s32[]{:S(2)}) async-start(), calls=%async_computation.12 | async-start | bytes 3244032
  436.5 59.2 %copy-start.6 = (bf16[384,128]{1,0:T(8,128)(2,1)S(1)}, bf16[384,128]{1,0:T(8,128)(2,1)}, u32[]{:S(2)}) copy-start(bf16[384,128]{1,0:T(8,128)(2,1)} %param.15) | copy-start | bytes 294916
  436.6 419.8 %reduce-scatter.11.cloned.1.call-start = ((), (), s32[]{:S(2)}) async-start(), calls=%async_computation.10 | async-start | bytes 1179648 | tf_op jit(solution)/shard_map/reduce_scatter | solution.py:88
  499.6 37.0 %copy-start = (bf16[384,4096]{1,0:T(8,128)(2,1)S(1)}, bf16[384,4096]{1,0:T(8,128)(2,1)}, u32[]{:S(2)}) copy-start(bf16[384,4096]{1,0:T(8,128)(2,1)} %all-gather.12.cloned.1.call-done) | copy-start | bytes 9437188
  505.1 253.6 %copy-start.10 = (f32[384]{0:T(512)S(1)}, f32[384]{0:T(512)}, u32[]{:S(2)}) copy-start(f32[384]{0:T(512)} %copy-done.9) | copy-start | bytes 4612
  505.1 253.6 %copy-start.12 = (f32[384]{0:T(512)S(1)}, f32[384]{0:T(512)}, u32[]{:S(2)}) copy-start(f32[384]{0:T(512)} %copy-done.11) | copy-start | bytes 4612
  505.1 253.6 %copy-start.37 = (f32[128]{0:T(128)S(1)}, f32[128]{0:T(128)}, u32[]{:S(2)}) copy-start(f32[128]{0:T(128)} %copy-done.36) | copy-start | bytes 1540
  505.1 326.1 %copy-start.71 = (f32[128]{0:T(128)S(1)}, f32[128]{0:T(128)}, u32[]{:S(2)}) copy-start(f32[128]{0:T(128)} %get-tuple-element.42) | copy-start | bytes 1540
  505.1 350.3 %copy-start.7 = (bf16[384,128]{1,0:T(8,128)(2,1)S(1)}, bf16[384,128]{1,0:T(8,128)(2,1)}, u32[]{:S(2)}) copy-start(bf16[384,128]{1,0:T(8,128)(2,1)} %param.15) | copy-start | bytes 294916
  (37 other events, 393.1 us)
Sparse Core Ops, SparseCore 0:
  9.9 27.1 all-gather.13
  38.9 25.7 all-gather.9
  89.2 72.2 all-gather.5
  163.2 26.1 all-gather.7
  193.1 219.3 reduce-scatter.12
  419.0 76.6 all-gather.11
  498.4 36.3 reduce-scatter.8
  539.2 218.4 reduce-scatter.14
  760.2 32.8 reduce-scatter.10
where the time goes:
time: 865 us; the launch traced here: 864 us
  waiting for transfers between devices  615 us (71%)
  blocking collectives  173 us (20%)
  matrix products  19.8 us (2%)
  other arithmetic  19.2 us (2%)
  local copies, waits for them, and re-layouts  16.5 us (2%)
  between operations  15 us (2%)
    unnamed x11, waiting for transfers between devices  435 us
    psum x1, blocking collectives, shards(): lax.psum((jnp.sum(wide, axis=1), jnp.sum(wide * wide, axis=1)), 'col')  76.2 us
    psum x1, blocking collectives, shards(): lax.psum((jnp.sum(hat_grad, axis=1), jnp.sum(hat_grad * centred, axis=1))...  72.2 us
    all_gather x1, waiting for transfers between devices, shards(): lax.all_gather((centred * local_gain[None, :]).astype(jnp.bfloat16), 'col...  64.5 us
    all_gather x1, waiting for transfers between devices, shards(): act_full = lax.all_gather(activated, 'col', axis=1, tiled=True)  58.9 us
    reduce_scatter x1, waiting for transfers between devices, shards(): lax.psum_scatter(contract_rows(normed, both_grads).astype(jnp.bfloat16),...  26.7 us
    all_gather x1, waiting for transfers between devices, shards(): lax.all_gather(w_value, 'row', axis=0, tiled=True)  24.6 us
    psum x1, blocking collectives, shards(): grad_kernel, grad_bias = lax.psum((kernel_term, bias_term), 'row')  24.2 us
  transfers between devices with their start and end apart: 13, of which 8 were waited for; matrix products, arithmetic and copies ran while one was open for 5% of the time, Pallas kernels for 0%

commit v1 on v0

--- a/solution.py
+++ b/solution.py
@@ -6,6 +6,12 @@
 K = 31
 LEN = 2048
 epsilon = 1e-05
+
+
+def gather_from_all(x, axis, dim):
+    peers = lax.axis_size(axis)
+    repeats = [peers if d == dim else 1 for d in range(x.ndim)]
+    return lax.all_to_all(jnp.tile(x, repeats), axis, split_axis=dim, concat_axis=dim, tiled=True)
 
 
 def extended(block, sides, width):
@@ -57,7 +63,7 @@
         (centred * local_gain[None, :]).astype(jnp.bfloat16), "col", axis=1, tiled=True
     )
     value_full, gate_full = (
-        lax.all_gather(w_value, "row", axis=0, tiled=True),
+        gather_from_all(w_value, "row", 0),
         lax.all_gather(w_gate, "row", axis=0, tiled=True),
     )
     value_pre = jnp.dot(normed, value_full, preferred_element_type=jnp.float32)

time: 865 us -> 835 us (0.965)
  waiting for transfers between devices: 615 us -> 584 us
    all_gather x1 -> x0, waiting for transfers between devices: 24.6 us -> none  [shards(): lax.all_gather(w_value, 'row', axis=0, tiled=True)]
    unnamed x11 -> x10, waiting for transfers between devices: 435 us -> 430 us
  transfers between devices with their start and end apart: 13 -> 13, of which waited for: 8 -> 7; matrix products, arithmetic and copies ran while one was open for 5% -> 5% of each run, Pallas kernels for 0% -> 0%
where the time goes in v1:
time: 835 us
  waiting for transfers between devices  584 us (70%)
  blocking collectives  173 us (21%)
  matrix products  19.6 us (2%)
  other arithmetic  17.5 us (2%)
  local copies, waits for them, and re-layouts  16.6 us (2%)
  between operations  14.8 us (2%)
  starting transfers between devices  9.96 us (1%)
    unnamed x10, waiting for transfers between devices  430 us
    psum x1, blocking collectives, shards(): lax.psum((jnp.sum(wide, axis=1), jnp.sum(wide * wide, axis=1)), 'col')  76.2 us
    psum x1, blocking collectives, shards(): lax.psum((jnp.sum(hat_grad, axis=1), jnp.sum(hat_grad * centred, axis=1))...  72.2 us
    all_gather x1, waiting for transfers between devices, shards(): lax.all_gather((centred * local_gain[None, :]).astype(jnp.bfloat16), 'col...  60.4 us
    all_gather x1, waiting for transfers between devices, shards(): act_full = lax.all_gather(activated, 'col', axis=1, tiled=True)  60.1 us
    reduce_scatter x1, waiting for transfers between devices, shards(): lax.psum_scatter(contract_rows(normed, both_grads).astype(jnp.bfloat16),...  26.7 us
    psum x1, blocking collectives, shards(): grad_kernel, grad_bias = lax.psum((kernel_term, bias_term), 'row')  24.2 us
  transfers between devices with their start and end apart: 13, of which 7 were waited for; matrix products, arithmetic and copies ran while one was open for 5% of the time, Pallas kernels for 0%

profile of v1, /device:TPU:0, one launch (start us, length us, event | category | flops | bytes accessed | tf_op | source)
XLA Modules:
  0.0 834.7 jit_solution(15311750616141069951)
XLA Ops:
  7.2 0.7 all-gather.11.cloned.1.call-update
  7.9 0.7 all-gather.7.cloned.1.call-update
  8.7 0.8 dynamic_slice.3
  9.5 1.1 convert_reduce_fusion.1
  10.5 76.2 %all-reduce.1 = (f32[384]{0:T(512)S(1)}, f32[384]{0:T(512)S(1)}) all-reduce(f32[384]{0:T(512)S(1)} %get-tuple-element.44, f32[384]{0:T(512)S(1)} %get-tuple-element.43), channel_id=1, replica_groups=mesh['row'=8,'col'=32] {'col'}, use_global_device_ids=true, to_apply=%region_3.0 | all-reduce | flops 768 | bytes 6144 | tf_op jit(solution)/shard_map/psum | solution.py:58
  86.8 0.6 copy-done.7
  87.3 1.7 fusion.16
  89.1 2.3 convolution_convert_fusion
  91.4 2.8 copy.16
  94.3 0.9 copy-done.6
  95.1 1.1 tile.2
  96.3 4.3 all-to-all-start
  101.0 60.4 %all-gather.5.cloned.1.call-done = bf16[384,4096]{1,0:T(8,128)(2,1)} async-done(((bf16[384,128]{1,0:T(8,128)(2,1)}), bf16[384,4096]{1,0:T(8,128)(2,1)}) %all-gather.5.cloned.1.call-update) | async-done | bytes 3145744 | tf_op jit(solution)/shard_map/all_gather | solution.py:62
  161.4 3.2 fusion.2
  164.6 2.9 multiply_convert_fusion.4
  167.5 1.3 collective-permute-start
  168.8 1.3 collective-permute-start.1
  170.3 3.3 collective-permute-done.1
  173.6 210.4 %reduce-scatter.13.cloned.1.call-done = bf16[128,384]{1,0:T(8,128)(2,1)} async-done(((bf16[4096,384]{1,0:T(8,128)(2,1)}), bf16[128,384]{1,0:T(8,128)(2,1)}) %reduce-scatter.13.cloned.1.call-update) | async-done | bytes 98320
  384.0 1.0 copy.17
  385.1 3.2 fusion.75
  388.3 0.7 multiply_convert_fusion.3
  389.4 1.3 collective-permute-start.2
  390.7 1.3 collective-permute-start.3
  392.1 3.3 collective-permute-done.3
  395.5 2.2 multiply_convert_fusion
  397.8 2.7 convolution_convert_fusion.1
  400.5 1.0 fusion.124
  401.5 0.2 copy-done.3
  401.7 1.0 add_convert_fusion
  402.7 2.8 copy.18
  405.6 0.2 reduce-scatter.11.cloned.1.call-start
  405.8 60.1 %all-gather.9.cloned.1.call-done = bf16[384,4096]{1,0:T(8,128)(2,1)} async-done(((bf16[384,128]{1,0:T(8,128)(2,1)}), bf16[384,4096]{1,0:T(8,128)(2,1)}) %all-gather.9.cloned.1.call-update) | async-done | bytes 3145744 | tf_op jit(solution)/shard_map/all_gather | solution.py:85
  465.9 3.9 convolution_convert_fusion.2
  469.8 1.7 fusion.73
  471.6 1.9 fusion.77
  473.4 1.8 fusion.79
  475.3 3.0 stack.127
  478.2 26.7 %reduce-scatter.9.cloned.1.call-done = bf16[512,256]{1,0:T(8,128)(2,1)} async-done(((bf16[4096,256]{1,0:T(8,128)(2,1)}), bf16[512,256]{1,0:T(8,128)(2,1)}) %reduce-scatter.9.cloned.1.call-update) | async-done | bytes 262160 | tf_op jit(solution)/shard_map/reduce_scatter | solution.py:130
  504.9 1.8 fusion.121
  506.7 2.9 fusion.3
  509.6 218.0 %reduce-scatter.15.cloned.1.call-done = bf16[128,384]{1,0:T(8,128)(2,1)} async-done(((bf16[4096,384]{1,0:T(8,128)(2,1)}), bf16[128,384]{1,0:T(8,128)(2,1)}) %reduce-scatter.15.cloned.1.call-update) | async-done | bytes 98320
  727.6 1.0 copy.19
  728.6 0.3 fusion.12
  728.9 72.2 %all-reduce = (f32[384]{0:T(512)S(1)}, f32[384]{0:T(512)S(1)}) all-reduce(f32[384]{0:T(512)S(1)} %get-tuple-element.40, f32[384]{0:T(512)S(1)} %get-tuple-element.41), channel_id=1, replica_groups=mesh['row'=8,'col'=32] {'col'}, use_global_device_ids=true, to_apply=%region_9.10 | all-reduce | flops 768 | bytes 6144 | tf_op jit(solution)/shard_map/psum | solution.py:143
  801.1 24.2 %all-reduce.2 = (f32[31,128]{1,0:T(8,128)}, f32[128]{0:T(128)}, f32[128]{0:T(128)}) all-reduce(f32[31,128]{1,0:T(8,128)S(1)} %stack.127, f32[128]{0:T(128)S(1)} %copy-done.36, f32[128]{0:T(128)S(1)} %get-tuple-element.39), channel_id=1, replica_groups=mesh['row'=8,'col'=32] {'row'}, use_global_device_ids=true, to_apply=%region_42.43 | all-reduce | flops 4224 | bytes 33792 | tf_op jit(solution)/shard_map/psum | solution.py:126
  825.3 0.9 fusion.10
  826.2 1.6 convert_element_type.92
  (110 shorter events, 1.3 us)
Async XLA Ops:
  7.2 82.0 %all-gather.11.cloned.1.call-start = ((), (), s32[]{:S(2)}) async-start(), calls=%async_computation.8 | async-start | bytes 1179648 | tf_op jit(solution)/shard_map/all_gather | solution.py:86
  7.9 93.1 %all-gather.7.cloned.1.call-start = ((), (), s32[]{:S(2)}) async-start(), calls=%async_computation.6 | async-start | bytes 1179648 | tf_op jit(solution)/shard_map/all_gather | solution.py:67
  8.7 152.8 %all-gather.5.cloned.1.call-start = ((), (), s32[]{:S(2)}) async-start(), calls=%async_computation.5 | async-start | bytes 3244032 | tf_op jit(solution)/shard_map/all_gather | solution.py:62
  9.5 79.6 %copy-start.34 = (f32[128]{0:T(128)}, f32[128]{0:T(128)S(1)}, u32[]{:S(2)}) copy-start(f32[128]{0:T(128)S(1)} %dynamic_slice.3) | copy-start | bytes 1540
  89.1 294.9 %reduce-scatter.13.cloned.1.call-start = ((), (), s32[]{:S(2)}) async-start(), calls=%async_computation.11 | async-start | bytes 3244032
  94.2 6.6 copy-start.33
  96.3 68.3 %all-to-all-start = ((bf16[8,512,128]{2,1,0:T(8,128)(2,1)}), bf16[8,512,128]{2,1,0:T(8,128)(2,1)S(1)}, u32[]{:S(2)}, u32[]{:S(2)}) async-start(bf16[8,512,128]{2,1,0:T(8,128)(2,1)} %tile.2), calls=%async_computation | async-start | bytes 2097152 | tf_op jit(solution)/shard_map/all_to_all | solution.py:14
  100.6 365.3 %all-gather.9.cloned.1.call-start = ((), (), s32[]{:S(2)}) async-start(), calls=%async_computation.7 | async-start | bytes 3244032 | tf_op jit(solution)/shard_map/all_gather | solution.py:85
  100.8 284.1 %copy-start.11 = (f32[384]{0:T(512)}, f32[384]{0:T(512)S(1)}, u32[]{:S(2)}) copy-start(f32[384]{0:T(512)S(1)} %get-tuple-element.77) | copy-start | bytes 4612
  100.9 284.1 %copy-start.12 = (f32[384]{0:T(512)}, f32[384]{0:T(512)S(1)}, u32[]{:S(2)}) copy-start(f32[384]{0:T(512)S(1)} %get-tuple-element.78) | copy-start | bytes 4612
  100.9 284.1 %copy-start.13 = (f32[384]{0:T(512)}, f32[384]{0:T(512)S(1)}, u32[]{:S(2)}) copy-start(f32[384]{0:T(512)S(1)} %get-tuple-element.91) | copy-start | bytes 4612
  100.9 284.1 %copy-start.14 = (f32[384]{0:T(512)}, f32[384]{0:T(512)S(1)}, u32[]{:S(2)}) copy-start(f32[384]{0:T(512)S(1)} %get-tuple-element.92) | copy-start | bytes 4612
  100.9 284.1 %copy-start.15 = (f32[384]{0:T(512)}, f32[384]{0:T(512)S(1)}, u32[]{:S(2)}) copy-start(f32[384]{0:T(512)S(1)} %get-tuple-element.93) | copy-start | bytes 4612
  100.9 284.1 %copy-start.16 = (f32[384]{0:T(512)}, f32[384]{0:T(512)S(1)}, u32[]{:S(2)}) copy-start(f32[384]{0:T(512)S(1)} %get-tuple-element.94) | copy-start | bytes 4612
  100.9 284.1 %copy-start.17 = (f32[384]{0:T(512)}, f32[384]{0:T(512)S(1)}, u32[]{:S(2)}) copy-start(f32[384]{0:T(512)S(1)} %get-tuple-element.76) | copy-start | bytes 4612
  100.9 284.1 %copy-start.18 = (f32[384]{0:T(512)}, f32[384]{0:T(512)S(1)}, u32[]{:S(2)}) copy-start(f32[384]{0:T(512)S(1)} %get-tuple-element.80) | copy-start | bytes 4612
  100.9 284.1 %copy-start.19 = (f32[384]{0:T(512)}, f32[384]{0:T(512)S(1)}, u32[]{:S(2)}) copy-start(f32[384]{0:T(512)S(1)} %get-tuple-element.81) | copy-start | bytes 4612
  100.9 284.1 %copy-start.20 = (f32[384]{0:T(512)}, f32[384]{0:T(512)S(1)}, u32[]{:S(2)}) copy-start(f32[384]{0:T(512)S(1)} %get-tuple-element.82) | copy-start | bytes 4612
  164.6 220.5 %copy-start.37 = (f32[128]{0:T(128)S(1)}, f32[128]{0:T(128)}, u32[]{:S(2)}) copy-start(f32[128]{0:T(128)} %param.13) | copy-start | bytes 1540
  167.5 2.8 collective-permute-start
  168.8 4.8 collective-permute-start.1
  170.2 218.1 %copy-start.21 = (f32[384]{0:T(512)}, f32[384]{0:T(512)S(1)}, u32[]{:S(2)}) copy-start(f32[384]{0:T(512)S(1)} %get-tuple-element.95) | copy-start | bytes 4612
  170.2 218.1 %copy-start.22 = (f32[384]{0:T(512)}, f32[384]{0:T(512)S(1)}, u32[]{:S(2)}) copy-start(f32[384]{0:T(512)S(1)} %get-tuple-element.100) | copy-start | bytes 4612
  170.2 218.1 %copy-start.23 = (f32[384]{0:T(512)}, f32[384]{0:T(512)S(1)}, u32[]{:S(2)}) copy-start(f32[384]{0:T(512)S(1)} %get-tuple-element.101) | copy-start | bytes 4612
  170.2 218.1 %copy-start.24 = (f32[384]{0:T(512)}, f32[384]{0:T(512)S(1)}, u32[]{:S(2)}) copy-start(f32[384]{0:T(512)S(1)} %get-tuple-element.102) | copy-start | bytes 4612
  170.2 218.1 %copy-start.25 = (f32[384]{0:T(512)}, f32[384]{0:T(512)S(1)}, u32[]{:S(2)}) copy-start(f32[384]{0:T(512)S(1)} %get-tuple-element.103) | copy-start | bytes 4612
  170.2 218.1 %copy-start.26 = (f32[384]{0:T(512)}, f32[384]{0:T(512)S(1)}, u32[]{:S(2)}) copy-start(f32[384]{0:T(512)S(1)} %get-tuple-element.104) | copy-start | bytes 4612
  170.2 218.1 %copy-start.27 = (f32[384]{0:T(512)}, f32[384]{0:T(512)S(1)}, u32[]{:S(2)}) copy-start(f32[384]{0:T(512)S(1)} %get-tuple-element.105) | copy-start | bytes 4612
  170.2 218.1 %copy-start.28 = (f32[384]{0:T(512)}, f32[384]{0:T(512)S(1)}, u32[]{:S(2)}) copy-start(f32[384]{0:T(512)S(1)} %get-tuple-element.106) | copy-start | bytes 4612
  170.2 218.1 %copy-start.29 = (f32[384]{0:T(512)}, f32[384]{0:T(512)S(1)}, u32[]{:S(2)}) copy-start(f32[384]{0:T(512)S(1)} %get-tuple-element.96) | copy-start | bytes 4612
  170.3 218.1 %copy-start.30 = (f32[384]{0:T(512)}, f32[384]{0:T(512)S(1)}, u32[]{:S(2)}) copy-start(f32[384]{0:T(512)S(1)} %get-tuple-element.97) | copy-start | bytes 4612
  170.3 218.1 %copy-start.31 = (f32[384]{0:T(512)}, f32[384]{0:T(512)S(1)}, u32[]{:S(2)}) copy-start(f32[384]{0:T(512)S(1)} %get-tuple-element.98) | copy-start | bytes 4612
  170.3 218.1 %copy-start.32 = (f32[384]{0:T(512)}, f32[384]{0:T(512)S(1)}, u32[]{:S(2)}) copy-start(f32[384]{0:T(512)S(1)} %get-tuple-element.99) | copy-start | bytes 4612
  389.1 115.8 %reduce-scatter.9.cloned.1.call-start = ((), (), s32[]{:S(2)}) async-start(), calls=%async_computation.9 | async-start | bytes 2359296 | tf_op jit(solution)/shard_map/reduce_scatter | solution.py:130
  389.4 2.7 collective-permute-start.2
  390.7 4.7 collective-permute-start.3
  395.5 2.3 copy-start.1
  400.4 327.2 %reduce-scatter.15.cloned.1.call-start = ((), (), s32[]{:S(2)}) async-start(), calls=%async_computation.12 | async-start | bytes 3244032
  400.5 1.2 copy-start.3
  405.5 60.4 %copy-start.4 = (bf16[384,128]{1,0:T(8,128)(2,1)S(1)}, bf16[384,128]{1,0:T(8,128)(2,1)}, u32[]{:S(2)}) copy-start(bf16[384,128]{1,0:T(8,128)(2,1)} %param.15) | copy-start | bytes 294916
  405.6 420.6 %reduce-scatter.11.cloned.1.call-start = ((), (), s32[]{:S(2)}) async-start(), calls=%async_computation.10 | async-start | bytes 1179648 | tf_op jit(solution)/shard_map/reduce_scatter | solution.py:94
  469.8 36.9 %copy-start = (bf16[384,4096]{1,0:T(8,128)(2,1)S(1)}, bf16[384,4096]{1,0:T(8,128)(2,1)}, u32[]{:S(2)}) copy-start(bf16[384,4096]{1,0:T(8,128)(2,1)} %all-gather.9.cloned.1.call-done) | copy-start | bytes 9437188
  469.8 36.9 %copy-start.2 = (bf16[384,128]{1,0:T(8,128)(2,1)S(1)}, bf16[384,128]{1,0:T(8,128)(2,1)}, u32[]{:S(2)}) copy-start(bf16[384,128]{1,0:T(8,128)(2,1)} %param.8) | copy-start | bytes 294916
  475.3 253.3 %copy-start.8 = (f32[384]{0:T(512)S(1)}, f32[384]{0:T(512)}, u32[]{:S(2)}) copy-start(f32[384]{0:T(512)} %copy-done.7) | copy-start | bytes 4612
  475.3 253.4 %copy-start.10 = (f32[384]{0:T(512)S(1)}, f32[384]{0:T(512)}, u32[]{:S(2)}) copy-start(f32[384]{0:T(512)} %copy-done.9) | copy-start | bytes 4612
  475.3 253.4 %copy-start.35 = (f32[128]{0:T(128)S(1)}, f32[128]{0:T(128)}, u32[]{:S(2)}) copy-start(f32[128]{0:T(128)} %copy-done.34) | copy-start | bytes 1540
  475.3 325.8 %copy-start.36 = (f32[128]{0:T(128)S(1)}, f32[128]{0:T(128)}, u32[]{:S(2)}) copy-start(f32[128]{0:T(128)} %get-tuple-element.42) | copy-start | bytes 1540
  475.3 350.0 %copy-start.5 = (bf16[384,128]{1,0:T(8,128)(2,1)S(1)}, bf16[384,128]{1,0:T(8,128)(2,1)}, u32[]{:S(2)}) copy-start(bf16[384,128]{1,0:T(8,128)(2,1)} %param.15) | copy-start | bytes 294916
  (3 other events, 2.1 us)
Sparse Core Ops, SparseCore 0:
  9.9 27.1 all-gather.10
  38.9 25.7 all-gather.6
  89.2 72.1 all-gather.4
  165.1 218.7 reduce-scatter.12
  389.2 76.6 all-gather.8
  468.5 36.3 reduce-scatter.8
  509.3 218.2 reduce-scatter.14
  730.1 32.9 reduce-scatter.10
